TPU v7x, 256 devices: a whole 4x4x8 slice. The times are simulated.
256 devices in a mesh: tm: 32 (over y, z), eval: 8 (over x, core).
Axes of the slice: x: 4, y: 4, z: 8, core: 2. Of those that a mesh axis runs over, the one named last changes fastest.
Arguments:
- hidden: bfloat16 [512, 1024, 1536], P('tm', 'eval'), may hold values from -9 to 9
- modulation: float32 [512, 2, 1536], P('tm'), may hold values from -2 to 3
- head_weight: bfloat16 [64, 1536], replicated, may hold values from -1 to 1
- real_score: bfloat16 [64, 21, 16, 4096], P('eval', None, None, 'tm'), may hold values from -152917 to 152917
- fake_score: bfloat16 [64, 21, 16, 4096], P('eval', None, None, 'tm'), may hold values from -152917 to 152917
- window_start: int32 [64], P('eval'), may hold values from 0 to 491, as said below
- timestep: int32 [64], P('eval'), may hold values from 20 to 999
Outputs:
- d_hidden: bfloat16 [512, 1024, 1536], P('tm', 'eval')
- head_grad: float32 [64, 1536], replicated
- mod_grad: float32 [512, 2, 1536], P('tm')
Inputs may be any that keep to these rules, and one draw needn't show every extreme that they name: `window_start`: every window lies inside the rollout; one window starts at frame 0 and one at the last possible frame.
All inputs are finite; a program needn't handle non-finite values.
Results may differ from a plain program's by a relative error of at most 0.0012.
The roundings to bfloat16 on the way count: a program that leaves them out, or rounds other values in their place, can miss the bound.
Values may be sent and summed in bfloat16 or wider, within the bound.
No kernel may reach another device: no remote copies, remote signals or barrier semaphores. Data moves between devices by JAX's collectives and lax.ppermute only.
A program may use at most 128 MiB of HBM per device.

v0:
```python
import jax
import jax.numpy as jnp
from jax import lax
from jax.experimental import pallas as pl
from jax.experimental.pallas import tpu as pltpu
from jax.sharding import PartitionSpec as P

C = 16
PATCH = 4
OUT = C * PATCH
WIN = 21
TOK = 1024
D = 1536
NTM = 32
NEV = 8
FD = 16
TD = TOK // NEV
PX = TD * PATCH
NF = FD * NTM
BLK = PX // PATCH
FG = 4
HG = 8
G = 2
ROW = 16
BROW = 32
PARTS = 2
NW = 8
HEAD_ROWS = OUT // NEV


F32 = jnp.float32
BF16 = jnp.bfloat16


def params(mib):
    return pltpu.CompilerParams(vmem_limit_bytes=mib * 1024 * 1024)


def dot(a, b, ca=1, cb=0):
    return lax.dot_general(a, b, (((ca,), (cb,)), ((), ())), preferred_element_type=F32)


def build_weight(w_ref, wp_ref):
    row = lax.broadcasted_iota(jnp.int32, (OUT, OUT), 0)
    col = lax.broadcasted_iota(jnp.int32, (OUT, OUT), 1)
    pick = (col == (row % C) * PATCH + row // C).astype(F32).astype(BF16)
    wp_ref[...] = dot(pick, w_ref[...]).astype(BF16)


def build_pixels(e_ref):
    row = lax.broadcasted_iota(jnp.int32, (PX, PX), 0)
    col = lax.broadcasted_iota(jnp.int32, (PX, PX), 1)
    e_ref[...] = (col == (row % TD) * PATCH + row // TD).astype(F32).astype(BF16)


def slot_turn():
    tm = lax.axis_index("tm")
    core = lax.axis_index("eval") % 2
    j, h = tm % 4, (tm // 4) % 2
    return jnp.where(h == core, j, 3 - j)


def forward_kernel(x_ref, mod_ref, w_ref, ad_ref, st_ref, lat_ref, wp_ref, e_ref):
    @pl.when(pl.program_id(0) == 0)
    def _():
        build_weight(w_ref, wp_ref)
        build_pixels(e_ref)

    turn = slot_turn()
    lane = lax.broadcasted_iota(jnp.int32, (ROW, 128), 1)
    for g in range(FG):
        scale = 1.0 + mod_ref[g, 1:2, :]
        shift = mod_ref[g, 0:1, :]
        for q in range(0, TD, ROW):
            x = x_ref[g, q : q + ROW, :].astype(F32)
            m = jnp.mean(x, axis=-1, keepdims=True)
            xc = x - m
            inv = lax.rsqrt(jnp.mean(xc * xc, axis=-1, keepdims=True) + 1e-06)
            st_ref[g, q : q + ROW, :] = jnp.where(lane == 0, m, inv)
            ad_ref[g, q : q + ROW, :] = ((xc * inv) * scale + shift).astype(BF16)
        o = dot(wp_ref[...], ad_ref[g], 1, 1).astype(BF16)
        wide = jnp.concatenate([o[s * C : (s + 1) * C] for s in range(PATCH)], axis=1)
        lat = dot(wide, e_ref[...]).astype(BF16)
        for k in range(4):
            lat_ref[lax.bitwise_xor(turn, k), g] = lat[:, k * BLK : (k + 1) * BLK]


def forward(hidden, modulation, weight):
    return pl.pallas_call(
        forward_kernel,
        grid=(FD // FG,),
        in_specs=[
            pl.BlockSpec((FG, TD, D), lambda i: (i, 0, 0)),
            pl.BlockSpec((FG, 2, D), lambda i: (i, 0, 0)),
            pl.BlockSpec((OUT, D), lambda i: (0, 0)),
        ],
        out_specs=[
            pl.BlockSpec((FG, TD, D), lambda i: (i, 0, 0)),
            pl.BlockSpec((FG, TD, 128), lambda i: (i, 0, 0)),
            pl.BlockSpec((4, FG, C, BLK), lambda i: (0, i, 0, 0)),
        ],
        out_shape=[
            jax.ShapeDtypeStruct((FD, TD, D), BF16),
            jax.ShapeDtypeStruct((FD, TD, 128), F32),
            jax.ShapeDtypeStruct((4, FD, C, BLK), BF16),
        ],
        scratch_shapes=[pltpu.VMEM((OUT, D), BF16), pltpu.VMEM((PX, PX), BF16)],
        compiler_params=params(56),
        name="forward",
    )(hidden, modulation, weight)


def row_tables(starts):
    tm = lax.axis_index("tm")
    ev = lax.axis_index("eval")
    y, zh, zj = tm // 8, (tm // 4) % 2, tm % 4
    x, core = ev // 2, ev % 2
    frame = starts[:, None] + jnp.arange(WIN, dtype=jnp.int32)[None, :]
    owner = frame // FD
    yo, ho, jo = owner // 8, (owner // 4) % 2, owner % 4
    slot = lax.bitwise_xor(lax.bitwise_xor(jo, zj), jnp.where(ho == zh, 0, 3))
    base = (NF // 2) * ((ho + core) % 2) + FD * slot + frame % FD
    block = (2 * y + 6 - yo) % 4
    return base + 64 * block, base + 64 * ((block + 4 - x) % 4)


def sums_kernel(row_ref, own_ref, other_ref, real_ref, out_ref):
    rows = []
    for w in range(NW):
        parts = []
        for t in range(WIN):
            row = row_ref[w, t]
            at = row % (NF // 2)
            latent = jnp.where(row < NF // 2, own_ref[at].astype(F32), other_ref[at].astype(F32))
            parts.append(jnp.abs(latent - real_ref[w, t].astype(F32)))
        while len(parts) > 1:
            parts = [a + b for a, b in zip(parts[::2], parts[1::2])] + ([parts[-1]] if len(parts) % 2 else [])
        rows.append(jnp.sum(parts[0], axis=0, keepdims=True))
    each = jnp.sum(jnp.concatenate(rows, axis=0), axis=1, keepdims=True)
    lane = lax.broadcasted_iota(jnp.int32, (NW, 128), 1)
    place = lax.broadcasted_iota(jnp.int32, (NW, 128), 0)
    total = jnp.sum(jnp.where(lane == place, each, 0.0), axis=0, keepdims=True)
    out_ref[...] = jnp.broadcast_to(total[None], (NTM, 1, 128))


def window_sums(rows, own, other, real):
    return pl.pallas_call(
        sums_kernel,
        in_specs=[
            pl.BlockSpec(memory_space=pltpu.SMEM),
            pl.BlockSpec(memory_space=pltpu.VMEM),
            pl.BlockSpec(memory_space=pltpu.VMEM),
            pl.BlockSpec(memory_space=pltpu.VMEM),
        ],
        out_specs=pl.BlockSpec(memory_space=pltpu.VMEM),
        out_shape=jax.ShapeDtypeStruct((NTM, 1, 128), F32),
        compiler_params=params(40),
        name="window_sums",
    )(rows, own, other, real)


def grads_kernel(row_ref, step_ref, tot_ref, real_ref, fake_ref, own_ref, other_ref, acc_ref, sem):
    lane = lax.broadcasted_iota(jnp.int32, (1, 128), 1)
    totals = jnp.sum(tot_ref[...], axis=0)
    normalizer = totals / (WIN * C * PATCH * TOK) + 1e-05
    level = jnp.zeros((1, 128), F32)
    for w in range(NW):
        level = jnp.where(lane == w, step_ref[w].astype(F32), level)
    weight = level / 1000.0 / normalizer
    acc_ref[...] = jnp.zeros_like(acc_ref)
    for w in range(NW):
        one = jnp.sum(jnp.where(lane == w, weight, 0.0), axis=1, keepdims=True)
        for t in range(WIN):
            acc_ref[row_ref[w, t]] += one * (fake_ref[w, t].astype(F32) - real_ref[w, t].astype(F32))
    copies = [
        pltpu.make_async_copy(acc_ref.at[pl.ds(NF // 2, NF // 2)], other_ref, sem.at[1]),
        pltpu.make_async_copy(acc_ref.at[pl.ds(0, NF // 2)], own_ref, sem.at[0]),
    ]
    for copy in copies:
        copy.start()
    for copy in copies:
        copy.wait()


def window_grads(rows, steps, totals, real, fake):
    smem = pl.BlockSpec(memory_space=pltpu.SMEM)
    vmem = pl.BlockSpec(memory_space=pltpu.VMEM)
    half = jax.ShapeDtypeStruct((NF // 2, C, BLK), F32)
    return pl.pallas_call(
        grads_kernel,
        in_specs=[smem, smem, vmem, vmem, vmem],
        out_specs=[pl.BlockSpec(memory_space=pl.ANY)] * 2,
        out_shape=[half, half],
        scratch_shapes=[pltpu.VMEM((NF, C, BLK), F32), pltpu.SemaphoreType.DMA((2,))],
        compiler_params=params(16),
        name="window_grads",
    )(rows, steps, totals, real, fake)


def holder(place):
    rel = (place >> 2) | (place & 2) | ((place & 1) << 2)
    return lax.bitwise_xor(lax.axis_index("eval"), rel)


def head_kernel(g_ref, ad_ref, up_ref, keep_ref, send_ref, e_ref, acc_ref):
    step = pl.program_id(0)

    @pl.when(step == 0)
    def _():
        build_pixels(e_ref)
        acc_ref[...] = jnp.zeros_like(acc_ref)

    turn = slot_turn()
    ups = []
    for g in range(HG):
        grad = jnp.concatenate([g_ref[lax.bitwise_xor(turn, k), g] for k in range(4)], axis=1)
        wide = dot(grad, e_ref[...], 1, 1).astype(BF16)
        up = jnp.concatenate([wide[:, s * TD : (s + 1) * TD] for s in range(PATCH)], axis=0)
        up_ref[g] = up
        ups.append(up)
    acc_ref[...] += dot(jnp.concatenate(ups, axis=1), ad_ref[...].reshape(HG * TD, D))

    @pl.when(step == pl.num_programs(0) - 1)
    def _():
        for place in range(NEV):
            e = holder(place)
            half = keep_ref if place < NEV // 2 else send_ref
            for i in range(HEAD_ROWS):
                row = (i % PATCH) * C + i // PATCH + (HEAD_ROWS // PATCH) * e
                half[place % (NEV // 2), i : i + 1, :] = acc_ref[pl.ds(row, 1), :]


def head_part(pieces, adapted):
    half = jax.ShapeDtypeStruct((NEV // 2, HEAD_ROWS, D), F32)
    return pl.pallas_call(
        head_kernel,
        grid=(FD // HG,),
        in_specs=[
            pl.BlockSpec((4, HG, C, BLK), lambda i: (0, i, 0, 0)),
            pl.BlockSpec((HG, TD, D), lambda i: (i, 0, 0)),
        ],
        out_specs=[pl.BlockSpec((HG, OUT, TD), lambda i: (i, 0, 0))]
        + [pl.BlockSpec((NEV // 2, HEAD_ROWS, D), lambda i: (0, 0, 0))] * 2,
        out_shape=[jax.ShapeDtypeStruct((FD, OUT, TD), BF16), half, half],
        scratch_shapes=[pltpu.VMEM((PX, PX), BF16), pltpu.VMEM((OUT, D), F32)],
        compiler_params=params(20),
        name="head_part",
    )(pieces, adapted)


def hidden_kernel(x_ref, st_ref, up_ref, mod_ref, w_ref, *refs):
    dh_ref, red_ref, wp_ref, da_ref = refs[-4:]

    @pl.when(pl.program_id(0) == 0)
    def _():
        build_weight(w_ref, wp_ref)

    for g in range(G):
        da_ref[...] = dot(up_ref[g], wp_ref[...], 0, 0)
        scale = 1.0 + mod_ref[g, 1:2, :]
        sum0 = jnp.zeros((BROW, D), F32)
        sum1 = jnp.zeros((BROW, D), F32)
        for q in range(0, TD, BROW):
            d_ad = da_ref[q : q + BROW, :]
            inv = st_ref[g, q : q + BROW, 1:2]
            normed = (x_ref[g, q : q + BROW, :].astype(F32) - st_ref[g, q : q + BROW, 0:1]) * inv
            product = d_ad * normed
            sum0 += d_ad
            sum1 += product
            dn = d_ad * scale
            m1 = jnp.mean(dn, axis=-1, keepdims=True)
            m2 = jnp.mean(product * scale, axis=-1, keepdims=True)
            dh_ref[g, q : q + BROW, :] = (inv * (dn - m1 - normed * m2)).astype(BF16)
        red_ref[g, 0:1, :] = jnp.sum(sum0, axis=0, keepdims=True)
        red_ref[g, 1:2, :] = jnp.sum(sum1, axis=0, keepdims=True)


def hidden_part(part, hidden, stats, up, modulation, weight, so_far, so_far_red):
    count = FD // PARTS // G
    at = part * count
    shapes = [jax.ShapeDtypeStruct((FD, TD, D), BF16), jax.ShapeDtypeStruct((FD, 2, D), F32)]
    more = [] if so_far is None else [so_far, so_far_red]
    return pl.pallas_call(
        hidden_kernel,
        grid=(count,),
        in_specs=[
            pl.BlockSpec((G, TD, D), lambda i: (i + at, 0, 0)),
            pl.BlockSpec((G, TD, 128), lambda i: (i + at, 0, 0)),
            pl.BlockSpec((G, OUT, TD), lambda i: (i + at, 0, 0)),
            pl.BlockSpec((G, 2, D), lambda i: (i + at, 0, 0)),
            pl.BlockSpec((OUT, D), lambda i: (0, 0)),
        ]
        + [pl.BlockSpec(memory_space=pl.ANY)] * len(more),
        out_specs=[
            pl.BlockSpec((G, TD, D), lambda i: (i + at, 0, 0)),
            pl.BlockSpec((G, 2, D), lambda i: (i + at, 0, 0)),
        ],
        out_shape=shapes,
        scratch_shapes=[pltpu.VMEM((OUT, D), BF16), pltpu.VMEM((TD, D), F32)],
        input_output_aliases={5: 0, 6: 1} if more else {},
        cost_estimate=pl.CostEstimate(
            flops=40 * FD // PARTS * TD * D, bytes_accessed=5 * FD // PARTS * TD * D, transcendentals=0
        ),
        compiler_params=params(16),
        name="hidden_part",
    )(hidden, stats, up, modulation, weight, *more)


def order_kernel(*refs):
    out_ref = refs[-1]
    place = 0
    for ref in refs[:-1]:
        for i in range(ref.shape[0]):
            at = pl.multiple_of(HEAD_ROWS * holder(place), HEAD_ROWS)
            out_ref[pl.ds(at, HEAD_ROWS), :] = ref[i]
            place += 1


def order_rows(blocks):
    vmem = pl.BlockSpec(memory_space=pltpu.VMEM)
    return pl.pallas_call(
        order_kernel,
        in_specs=[vmem] * len(blocks),
        out_specs=vmem,
        out_shape=jax.ShapeDtypeStruct((OUT, D), F32),
        compiler_params=params(4),
        name="order_rows",
    )(*blocks)


def far_pairs():
    pairs = []
    for tm in range(NTM):
        for ev in range(NEV):
            y, z = divmod(tm, 8)
            x, c = divmod(ev, 2)
            h, j = divmod(z, 4)
            dest_tm = 8 * x + 4 * c + (j if h == c else 3 - j)
            dest_ev = 2 * ((2 * x - y + 2) % 4) + h
            pairs.append((tm * NEV + ev, dest_tm * NEV + dest_ev))
    return pairs


def x_step(value, steps):
    return lax.ppermute(value, "eval", [(i, (i + 2 * steps) % NEV) for i in range(NEV)])


def near(slots):
    return [slots[0]] + [lax.ppermute(slots[q], "tm", [(i, i ^ q) for i in range(NTM)]) for q in (1, 2, 3)]


def eval_flip(value, bit):
    return lax.ppermute(value, "eval", [(i, i ^ bit) for i in range(NEV)])


def swap4(value, axis, groups):
    return lax.all_to_all(value, axis, split_axis=0, concat_axis=0, tiled=True, axis_index_groups=groups)


X_GROUPS = [[0, 2, 4, 6], [1, 3, 5, 7]]


def per_device(hidden, modulation, head_weight, real_score, fake_score, window_start, timestep):
    both = ("tm", "eval")
    rows, grad_rows = row_tables(window_start)
    adapted, stats, pieces = forward(hidden, modulation, head_weight)
    held = jnp.concatenate(near(lax.ppermute(pieces, both, far_pairs())), axis=0)
    own = swap4(jnp.broadcast_to(held[None], (4, 64, C, BLK)), "eval", X_GROUPS).reshape(NF // 2, C, BLK)
    other = eval_flip(own, 1)
    sums = window_sums(rows, own, other, real_score)
    totals = lax.all_to_all(sums, "tm", split_axis=0, concat_axis=0, tiled=True)
    keep, give = window_grads(grad_rows, timestep, totals, real_score, fake_score)
    got = eval_flip(give, 1)

    def half(i):
        return keep[32 * i : 32 * (i + 1)] + got[32 * i : 32 * (i + 1)]

    four = lax.optimization_barrier((half(4), half(5), half(3), half(6)))
    ahead = x_step(four[0], 1)
    behind = x_step(four[1], -1)
    ahead_direct = x_step(four[2], 1)
    behind_direct = x_step(four[3], -1)
    ahead = x_step(lax.optimization_barrier(half(2) + ahead), 1)
    behind = x_step(lax.optimization_barrier(half(7) + behind), -1)
    mine = [half(0) + behind_direct + ahead, half(1) + ahead_direct + behind]
    mine = jnp.concatenate(mine, axis=0).astype(BF16).reshape(4, FD, C, BLK)
    back = jnp.stack(near(mine), axis=0)
    pieces = lax.ppermute(back, both, [(b, a) for a, b in far_pairs()])
    up, head, send = head_part(pieces, adapted)
    for bit, size in ((1, 4), (2, 2), (4, 1)):
        total = head + eval_flip(send, bit)
        head, send = total[: size // 2], total[size // 2 :]
    head = total
    d_hidden = mod_grad = None
    for part in range(PARTS):
        d_hidden, mod_grad = hidden_part(
            part, hidden, stats, up, modulation, head_weight, d_hidden, mod_grad
        )
    for bit in (1, 2, 4):
        mod_grad = mod_grad + eval_flip(mod_grad, bit)
    for bit in (1, 2, 4, 8, 16):
        moved = lax.ppermute(head, "tm", [(i, i ^ bit) for i in range(NTM)])
        head = head + moved
    blocks = [head]
    for bit in (4, 2, 1):
        blocks.append(eval_flip(jnp.concatenate(blocks, axis=0), bit))
    return (d_hidden, order_rows(blocks), mod_grad)


def solution(mesh):
    placed = (
        P("tm", "eval", None),
        P("tm", None, None),
        P(),
        P("eval", None, None, "tm"),
        P("eval", None, None, "tm"),
        P("eval"),
        P("eval"),
    )
    return jax.shard_map(
        per_device,
        mesh=mesh,
        in_specs=placed,
        out_specs=(P("tm", "eval", None), P(), P("tm", None, None)),
        check_vma=False,
    )
```

profile of v0, /device:TPU:34, one launch (start us, length us, event | category | flops | bytes accessed | tf_op | source)
XLA Modules:
  0.0 191.6 jit_solution(18258254913178970524)
XLA Ops:
  0.6 11.7 %forward.1 = (bf16[16,128,1536]{2,1,0:T(8,128)(2,1)}, f32[16,128,128]{2,1,0:T(8,128)}, bf16[4,16,16,128]{3,2,1,0:T(8,128)(2,1)}) custom-call(bf16[16,128,1536]{2,1,0:T(8,128)(2,1)} %x_ref.5, f32[16,2,1536]{2,1,0:T(2,128)} %mod_ref.5, bf16[64,1536]{1,0:T(8,128)(2,1)} %w_ref.5), custom_call_target="tpu_custom_call" | custom-call | tf_op jit(solution)/shard_map/forward/pallas_call | solution.py:89
  13.9 5.9 %collective-permute-done = bf16[4,16,16,128]{3,2,1,0:T(8,128)(2,1)S(1)} collective-permute-done((bf16[4,16,16,128]{3,2,1,0:T(8,128)(2,1)}, bf16[4,16,16,128]{3,2,1,0:T(8,128)(2,1)S(1)}, u32[]{:S(2)}, u32[]{:S(2)}) %collective-permute-start) | collective-permute-done | bytes 262176 | tf_op jit(solution)/shard_map/ppermute | solution.py:367
  29.1 20.8 %all_to_all.10 = bf16[4,64,16,128]{3,2,1,0:T(8,128)(2,1)S(1)} all-to-all(bf16[4,64,16,128]{3,2,1,0:T(8,128)(2,1)S(1)} %broadcast_in_dim.6), channel_id=1, replica_groups={{0,2,4,6},{1,3,5,7},{8,10,12,14},{9,11,13,15},{16,18,20,22},{17,19,21,2..., dimensions={0} | all-to-all | bytes 2097152 | tf_op jit(solution)/shard_map/all_to_all | solution.py:357
  51.1 2.2 %collective-permute-done.4.other_ref = bf16[256,16,128]{2,1,0:T(8,128)(2,1)S(1)} collective-permute-done((bf16[256,16,128]{2,1,0:T(8,128)(2,1)S(1)}, bf16[256,16,128]{2,1,0:T(8,128)(2,1)S(1)}, u32[]{:S(2)}, u32[]{:S(2)}) %collective-permute-start.4) | collective-permute-done | bytes 1048608 | tf_op jit(solution)/shard_map/ppermute | solution.py:353
  54.9 16.0 %all_to_all.11.tot_ref = f32[32,1,128]{2,1,0:T(1,128)S(1)} all-to-all(f32[32,1,128]{2,1,0:T(1,128)S(1)} %window_sums.1), channel_id=1, replica_groups=mesh['tm'=32,'eval'=8] {'tm'}, dimensions={0} | all-to-all | bytes 32768 | tf_op jit(solution)/shard_map/all_to_all | solution.py:371
  73.0 4.1 %collective-permute-done.5 = f32[256,16,128]{2,1,0:T(8,128)S(1)} collective-permute-done((f32[256,16,128]{2,1,0:T(8,128)S(1)}, f32[256,16,128]{2,1,0:T(8,128)S(1)}, u32[]{:S(2)}, u32[]{:S(2)}) %collective-permute-start.5) | collective-permute-done | bytes 2097184 | tf_op jit(solution)/shard_map/ppermute | solution.py:353
  79.5 2.7 %collective-permute-start.11 = (f32[32,16,128]{2,1,0:T(8,128)S(1)}, f32[32,16,128]{2,1,0:T(8,128)S(1)}, u32[]{:S(2)}, u32[]{:S(2)}) collective-permute-start(f32[32,16,128]{2,1,0:T(8,128)S(1)} %get-tuple-element.26), channel_id=1, source_target_pairs={{0,6},{1,7},{2,0},{3,1},{4,2},{5,3},{6,4},{7,5},{8,14},{9,15},{10,... | collective-permute-start | bytes 786440 | tf_op jit(solution)/shard_map/ppermute | solution.py:345
  82.1 3.6 %collective-permute-done.7 = f32[32,16,128]{2,1,0:T(8,128)S(1)} collective-permute-done((f32[32,16,128]{2,1,0:T(8,128)S(1)}, f32[32,16,128]{2,1,0:T(8,128)S(1)}, u32[]{:S(2)}, u32[]{:S(2)}) %collective-permute-start.7) | collective-permute-done | bytes 262176 | tf_op jit(solution)/shard_map/ppermute | solution.py:345
  88.0 3.5 %collective-permute-done.11 = f32[32,16,128]{2,1,0:T(8,128)S(1)} collective-permute-done((f32[32,16,128]{2,1,0:T(8,128)S(1)}, f32[32,16,128]{2,1,0:T(8,128)S(1)}, u32[]{:S(2)}, u32[]{:S(2)}) %collective-permute-start.11) | collective-permute-done | bytes 262176 | tf_op jit(solution)/shard_map/ppermute | solution.py:345
  91.5 4.3 %collective-permute-done.8 = f32[32,16,128]{2,1,0:T(8,128)S(1)} collective-permute-done((f32[32,16,128]{2,1,0:T(8,128)S(1)}, f32[32,16,128]{2,1,0:T(8,128)S(1)}, u32[]{:S(2)}, u32[]{:S(2)}) %collective-permute-start.8) | collective-permute-done | bytes 262176 | tf_op jit(solution)/shard_map/ppermute | solution.py:345
  95.9 3.3 %collective-permute-start.12 = (f32[32,16,128]{2,1,0:T(8,128)S(1)}, f32[32,16,128]{2,1,0:T(8,128)S(1)}, u32[]{:S(2)}, u32[]{:S(2)}) collective-permute-start(f32[32,16,128]{2,1,0:T(8,128)S(1)} %get-tuple-element.36), channel_id=1, source_target_pairs={{0,6},{1,7},{2,0},{3,1},{4,2},{5,3},{6,4},{7,5},{8,14},{9,15},{10,... | collective-permute-start | bytes 786440 | tf_op jit(solution)/shard_map/ppermute | solution.py:345
  100.7 2.4 %collective-permute-done.12 = f32[32,16,128]{2,1,0:T(8,128)S(1)} collective-permute-done((f32[32,16,128]{2,1,0:T(8,128)S(1)}, f32[32,16,128]{2,1,0:T(8,128)S(1)}, u32[]{:S(2)}, u32[]{:S(2)}) %collective-permute-start.12) | collective-permute-done | bytes 262176 | tf_op jit(solution)/shard_map/ppermute | solution.py:345
  103.9 2.3 %collective-permute-start.14 = (bf16[16,16,128]{2,1,0:T(8,128)(2,1)S(1)}, bf16[16,16,128]{2,1,0:T(8,128)(2,1)S(1)}, u32[]{:S(2)}, u32[]{:S(2)}) collective-permute-start(bf16[16,16,128]{2,1,0:T(8,128)(2,1)S(1)} %get-tuple-element.48), channel_id=1, source_target_pairs={{0,24},{8,16},{16,8},{24,0},{32,56},{40,48},{48,40},{56,32},{64,88... | collective-permute-start | bytes 196616 | tf_op jit(solution)/shard_map/ppermute | solution.py:349
  106.2 2.4 %collective-permute-done.13 = bf16[16,16,128]{2,1,0:T(8,128)(2,1)S(1)} collective-permute-done((bf16[16,16,128]{2,1,0:T(8,128)(2,1)S(1)}, bf16[16,16,128]{2,1,0:T(8,128)(2,1)S(1)}, u32[]{:S(2)}, u32[]{:S(2)}) %collective-permute-start.13) | collective-permute-done | bytes 65568 | tf_op jit(solution)/shard_map/ppermute | solution.py:349
  110.5 2.6 %collective-permute-start.15 = (bf16[4,16,16,128]{3,2,1,0:T(8,128)(2,1)S(1)}, bf16[4,16,16,128]{3,2,1,0:T(8,128)(2,1)S(1)}, u32[]{:S(2)}, u32[]{:S(2)}) collective-permute-start(bf16[4,16,16,128]{3,2,1,0:T(8,128)(2,1)S(1)} %pad_maximum_fusion.1), channel_id=1, source_target_pairs={{4,0},{60,1},{64,2},{120,3},{132,4},{188,5},{192,6},{248,7},{12,8}... | collective-permute-start | bytes 786440 | tf_op jit(solution)/shard_map/ppermute | solution.py:388
  113.1 9.1 %collective-permute-done.15.g_ref = bf16[4,16,16,128]{3,2,1,0:T(8,128)(2,1)S(1)} collective-permute-done((bf16[4,16,16,128]{3,2,1,0:T(8,128)(2,1)S(1)}, bf16[4,16,16,128]{3,2,1,0:T(8,128)(2,1)S(1)}, u32[]{:S(2)}, u32[]{:S(2)}) %collective-permute-start.15) | collective-permute-done | bytes 262176 | tf_op jit(solution)/shard_map/ppermute | solution.py:388
  122.3 3.9 %head_part.1 = (bf16[16,64,128]{2,1,0:T(8,128)(2,1)S(1)}, f32[4,8,1536]{2,1,0:T(8,128)S(1)}, f32[4,8,1536]{2,1,0:T(8,128)S(1)}) custom-call(bf16[4,16,16,128]{3,2,1,0:T(8,128)(2,1)S(1)} %collective-permute-done.15.g_ref, bf16[16,128,1536]{2,1,0:T(8,128)(2,1)S(1)} %bitcast.17), custom_call_target="tpu_custom_call" | custom-call | tf_op jit(solution)/shard_map/head_part/pallas_call | solution.py:235
  127.8 3.2 %collective-permute-start.17 = (f32[2,8,1536]{2,1,0:T(8,128)S(1)}, f32[2,8,1536]{2,1,0:T(8,128)S(1)}, u32[]{:S(2)}, u32[]{:S(2)}) collective-permute-start(f32[2,8,1536]{2,1,0:T(8,128)S(1)} %slice.140), channel_id=1, source_target_pairs={{0,2},{1,3},{2,0},{3,1},{4,6},{5,7},{6,4},{7,5},{8,10},{9,11},{10,... | collective-permute-start | bytes 294920 | tf_op jit(solution)/shard_map/ppermute | solution.py:353
  131.0 3.1 %collective-permute-done.17 = f32[2,8,1536]{2,1,0:T(8,128)S(1)} collective-permute-done((f32[2,8,1536]{2,1,0:T(8,128)S(1)}, f32[2,8,1536]{2,1,0:T(8,128)S(1)}, u32[]{:S(2)}, u32[]{:S(2)}) %collective-permute-start.17) | collective-permute-done | bytes 98336 | tf_op jit(solution)/shard_map/ppermute | solution.py:353
  134.1 5.0 %collective-permute-start.18 = (f32[1,8,1536]{2,1,0:T(8,128)S(1)}, f32[1,8,1536]{2,1,0:T(8,128)S(1)}, u32[]{:S(2)}, u32[]{:S(2)}) collective-permute-start(f32[1,8,1536]{2,1,0:T(8,128)S(1)} %slice.142), channel_id=1, source_target_pairs={{0,4},{1,5},{2,6},{3,7},{4,0},{5,1},{6,2},{7,3},{8,12},{9,13},{10,... | collective-permute-start | bytes 147464 | tf_op jit(solution)/shard_map/ppermute | solution.py:353
  139.1 2.1 %collective-permute-done.18 = f32[1,8,1536]{2,1,0:T(8,128)S(1)} collective-permute-done((f32[1,8,1536]{2,1,0:T(8,128)S(1)}, f32[1,8,1536]{2,1,0:T(8,128)S(1)}, u32[]{:S(2)}, u32[]{:S(2)}) %collective-permute-start.18) | collective-permute-done | bytes 49184 | tf_op jit(solution)/shard_map/ppermute | solution.py:353
  142.5 2.8 %collective-permute-done.19 = f32[1,8,1536]{2,1,0:T(8,128)S(1)} collective-permute-done((f32[1,8,1536]{2,1,0:T(8,128)S(1)}, f32[1,8,1536]{2,1,0:T(8,128)S(1)}, u32[]{:S(2)}, u32[]{:S(2)}) %collective-permute-start.19) | collective-permute-done | bytes 49184 | tf_op jit(solution)/shard_map/ppermute | solution.py:402
  145.3 2.6 %collective-permute-start.20 = (f32[1,8,1536]{2,1,0:T(8,128)S(1)}, f32[1,8,1536]{2,1,0:T(8,128)S(1)}, u32[]{:S(2)}, u32[]{:S(2)}) collective-permute-start(f32[1,8,1536]{2,1,0:T(8,128)S(1)} %add.192), channel_id=1, source_target_pairs={{0,16},{8,24},{16,0},{24,8},{32,48},{40,56},{48,32},{56,40},{64,80... | collective-permute-start | bytes 147464 | tf_op jit(solution)/shard_map/ppermute | solution.py:402
  148.0 5.3 %hidden_part.2 = (bf16[16,128,1536]{2,1,0:T(8,128)(2,1)}, f32[16,2,1536]{2,1,0:T(2,128)S(1)}) custom-call(bf16[16,128,1536]{2,1,0:T(8,128)(2,1)S(1)} %bitcast.15, f32[16,128,128]{2,1,0:T(8,128)S(1)} %copy-done, bf16[16,64,128]{2,1,0:T(8,128)(2,1)S(1)} %get-tuple-element.28.up_ref, f32[16,2,1536]{2,1,0:T(2,128)S(1)} %copy-done.2, bf16[64,1536]{1,0:T(8,128)(2,1)S(1)} %copy-done.3), custom_call_target="tpu_custom_call" | custom-call | flops 62914560 | bytes 7864320 | tf_op jit(solution)/shard_map/hidden_part/pallas_call | solution.py:283
  153.8 5.2 %hidden_part.3 = (bf16[16,128,1536]{2,1,0:T(8,128)(2,1)}, f32[16,2,1536]{2,1,0:T(2,128)S(1)}) custom-call(bf16[16,128,1536]{2,1,0:T(8,128)(2,1)S(1)} %bitcast.15, f32[16,128,128]{2,1,0:T(8,128)S(1)} %copy-done, bf16[16,64,128]{2,1,0:T(8,128)(2,1)S(1)} %get-tuple-element.28.up_ref, ...), custom_call_target="tpu_custom_call", output_to_operand_aliasing={{0}: (5, {}), {1}: (6, {})} | custom-call | flops 62914560 | bytes 7864320 | tf_op jit(solution)/shard_map/hidden_part/pallas_call | solution.py:283
  159.1 2.4 %collective-permute-done.21 = f32[1,8,1536]{2,1,0:T(8,128)S(1)} collective-permute-done((f32[1,8,1536]{2,1,0:T(8,128)S(1)}, f32[1,8,1536]{2,1,0:T(8,128)S(1)}, u32[]{:S(2)}, u32[]{:S(2)}) %collective-permute-start.21) | collective-permute-done | bytes 49184 | tf_op jit(solution)/shard_map/ppermute | solution.py:402
  161.5 4.1 %collective-permute-done.22 = f32[1,8,1536]{2,1,0:T(8,128)S(1)} collective-permute-done((f32[1,8,1536]{2,1,0:T(8,128)S(1)}, f32[1,8,1536]{2,1,0:T(8,128)S(1)}, u32[]{:S(2)}, u32[]{:S(2)}) %collective-permute-start.22) | collective-permute-done | bytes 49184 | tf_op jit(solution)/shard_map/ppermute | solution.py:402
  165.6 4.0 %collective-permute-start.23 = (f32[1,8,1536]{2,1,0:T(8,128)S(1)}, f32[1,8,1536]{2,1,0:T(8,128)S(1)}, u32[]{:S(2)}, u32[]{:S(2)}) collective-permute-start(f32[1,8,1536]{2,1,0:T(8,128)S(1)} %add.195), channel_id=1, source_target_pairs={{0,128},{8,136},{16,144},{24,152},{32,160},{40,168},{48,176},{56,1... | collective-permute-start | bytes 147464 | tf_op jit(solution)/shard_map/ppermute | solution.py:402
  169.6 2.1 %collective-permute-done.23 = f32[1,8,1536]{2,1,0:T(8,128)S(1)} collective-permute-done((f32[1,8,1536]{2,1,0:T(8,128)S(1)}, f32[1,8,1536]{2,1,0:T(8,128)S(1)}, u32[]{:S(2)}, u32[]{:S(2)}) %collective-permute-start.23) | collective-permute-done | bytes 49184 | tf_op jit(solution)/shard_map/ppermute | solution.py:402
  171.7 3.8 %collective-permute-start.24 = (f32[1,8,1536]{2,1,0:T(8,128)S(1)}, f32[1,8,1536]{2,1,0:T(8,128)S(1)}, u32[]{:S(2)}, u32[]{:S(2)}) collective-permute-start(f32[1,8,1536]{2,1,0:T(8,128)S(1)} %add.196.refs_0_), channel_id=1, source_target_pairs={{0,4},{1,5},{2,6},{3,7},{4,0},{5,1},{6,2},{7,3},{8,12},{9,13},{10,... | collective-permute-start | bytes 147464 | tf_op jit(solution)/shard_map/ppermute | solution.py:353
  179.7 3.0 %collective-permute-done.28 = f32[16,2,1536]{2,1,0:T(2,128)S(1)} collective-permute-done((f32[16,2,1536]{2,1,0:T(2,128)S(1)}, f32[16,2,1536]{2,1,0:T(2,128)S(1)}, u32[]{:S(2)}, u32[]{:S(2)}) %collective-permute-start.28) | collective-permute-done | bytes 196640 | tf_op jit(solution)/shard_map/ppermute | solution.py:353
  183.9 6.2 %collective-permute-done.29 = f32[16,2,1536]{2,1,0:T(2,128)S(1)} collective-permute-done((f32[16,2,1536]{2,1,0:T(2,128)S(1)}, f32[16,2,1536]{2,1,0:T(2,128)S(1)}, u32[]{:S(2)}, u32[]{:S(2)}) %collective-permute-start.29) | collective-permute-done | bytes 196640 | tf_op jit(solution)/shard_map/ppermute | solution.py:353
  (87 shorter events, 35.1 us)
Async XLA Ops:
  12.4 7.5 %collective-permute-start = (bf16[4,16,16,128]{3,2,1,0:T(8,128)(2,1)}, bf16[4,16,16,128]{3,2,1,0:T(8,128)(2,1)S(1)}, u32[]{:S(2)}, u32[]{:S(2)}) collective-permute-start(bf16[4,16,16,128]{3,2,1,0:T(8,128)(2,1)} %get-tuple-element.20), channel_id=1, source_target_pairs={{0,4},{1,60},{2,64},{3,120},{4,132},{5,188},{6,192},{7,248},{8,12}... | collective-permute-start | bytes 786440 | tf_op jit(solution)/shard_map/ppermute | solution.py:367
  19.9 5.4 %collective-permute-start.3 = (bf16[16,16,128]{2,1,0:T(8,128)(2,1)S(1)}, bf16[16,16,128]{2,1,0:T(8,128)(2,1)S(1)}, u32[]{:S(2)}, u32[]{:S(2)}) collective-permute-start(bf16[16,16,128]{2,1,0:T(8,128)(2,1)S(1)} %get-tuple-element.42), channel_id=1, source_target_pairs={{0,24},{8,16},{16,8},{24,0},{32,56},{40,48},{48,40},{56,32},{64,88... | collective-permute-start | bytes 196616 | tf_op jit(solution)/shard_map/ppermute | solution.py:349
  21.9 5.2 %collective-permute-start.2 = (bf16[16,16,128]{2,1,0:T(8,128)(2,1)S(1)}, bf16[16,16,128]{2,1,0:T(8,128)(2,1)S(1)}, u32[]{:S(2)}, u32[]{:S(2)}) collective-permute-start(bf16[16,16,128]{2,1,0:T(8,128)(2,1)S(1)} %get-tuple-element.43), channel_id=1, source_target_pairs={{0,16},{8,24},{16,0},{24,8},{32,48},{40,56},{48,32},{56,40},{64,80... | collective-permute-start | bytes 196616 | tf_op jit(solution)/shard_map/ppermute | solution.py:349
  23.9 5.1 %collective-permute-start.1 = (bf16[16,16,128]{2,1,0:T(8,128)(2,1)S(1)}, bf16[16,16,128]{2,1,0:T(8,128)(2,1)S(1)}, u32[]{:S(2)}, u32[]{:S(2)}) collective-permute-start(bf16[16,16,128]{2,1,0:T(8,128)(2,1)S(1)} %get-tuple-element.44), channel_id=1, source_target_pairs={{0,8},{8,0},{16,24},{24,16},{32,40},{40,32},{48,56},{56,48},{64,72... | collective-permute-start | bytes 196616 | tf_op jit(solution)/shard_map/ppermute | solution.py:349
  49.9 3.3 %collective-permute-start.4 = (bf16[256,16,128]{2,1,0:T(8,128)(2,1)S(1)}, bf16[256,16,128]{2,1,0:T(8,128)(2,1)S(1)}, u32[]{:S(2)}, u32[]{:S(2)}) collective-permute-start(bf16[256,16,128]{2,1,0:T(8,128)(2,1)S(1)} %bitcast.18), channel_id=1, source_target_pairs={{0,1},{1,0},{2,3},{3,2},{4,5},{5,4},{6,7},{7,6},{8,9},{9,8},{10,11... | collective-permute-start | bytes 3145736 | tf_op jit(solution)/shard_map/ppermute | solution.py:353
  53.2 69.0 %slice-start.2 = ((s8[6291456]{0:T(1024)(128)(4,1)}), s8[2097152]{0:T(1024)(128)(4,1)S(1)}, s32[]{:S(2)}) async-start(s8[6291456]{0:T(1024)(128)(4,1)} %bitcast.16), calls=%async_computation.4 | async-start | bytes 4194304
  72.9 4.2 %collective-permute-start.5 = (f32[256,16,128]{2,1,0:T(8,128)S(1)}, f32[256,16,128]{2,1,0:T(8,128)S(1)}, u32[]{:S(2)}, u32[]{:S(2)}) collective-permute-start(f32[256,16,128]{2,1,0:T(8,128)S(1)} %get-tuple-element.22), channel_id=1, source_target_pairs={{0,1},{1,0},{2,3},{3,2},{4,5},{5,4},{6,7},{7,6},{8,9},{9,8},{10,11... | collective-permute-start | bytes 6291464 | tf_op jit(solution)/shard_map/ppermute | solution.py:353
  77.4 8.4 %collective-permute-start.7 = (f32[32,16,128]{2,1,0:T(8,128)S(1)}, f32[32,16,128]{2,1,0:T(8,128)S(1)}, u32[]{:S(2)}, u32[]{:S(2)}) collective-permute-start(f32[32,16,128]{2,1,0:T(8,128)S(1)} %get-tuple-element.24), channel_id=1, source_target_pairs={{0,2},{1,3},{2,4},{3,5},{4,6},{5,7},{6,0},{7,1},{8,10},{9,11},{10,... | collective-permute-start | bytes 786440 | tf_op jit(solution)/shard_map/ppermute | solution.py:345
  77.7 10.3 %collective-permute-start.6 = (f32[32,16,128]{2,1,0:T(8,128)S(1)}, f32[32,16,128]{2,1,0:T(8,128)S(1)}, u32[]{:S(2)}, u32[]{:S(2)}) collective-permute-start(f32[32,16,128]{2,1,0:T(8,128)S(1)} %get-tuple-element.23), channel_id=1, source_target_pairs={{0,6},{1,7},{2,0},{3,1},{4,2},{5,3},{6,4},{7,5},{8,14},{9,15},{10,... | collective-permute-start | bytes 786440 | tf_op jit(solution)/shard_map/ppermute | solution.py:345
  79.5 12.0 %collective-permute-start.11 = (f32[32,16,128]{2,1,0:T(8,128)S(1)}, f32[32,16,128]{2,1,0:T(8,128)S(1)}, u32[]{:S(2)}, u32[]{:S(2)}) collective-permute-start(f32[32,16,128]{2,1,0:T(8,128)S(1)} %get-tuple-element.26), channel_id=1, source_target_pairs={{0,6},{1,7},{2,0},{3,1},{4,2},{5,3},{6,4},{7,5},{8,14},{9,15},{10,... | collective-permute-start | bytes 786440 | tf_op jit(solution)/shard_map/ppermute | solution.py:345
  85.9 9.9 %collective-permute-start.8 = (f32[32,16,128]{2,1,0:T(8,128)S(1)}, f32[32,16,128]{2,1,0:T(8,128)S(1)}, u32[]{:S(2)}, u32[]{:S(2)}) collective-permute-start(f32[32,16,128]{2,1,0:T(8,128)S(1)} %fusion.4), channel_id=1, source_target_pairs={{0,2},{1,3},{2,4},{3,5},{4,6},{5,7},{6,0},{7,1},{8,10},{9,11},{10,... | collective-permute-start | bytes 786440 | tf_op jit(solution)/shard_map/ppermute | solution.py:345
  86.2 14.5 %collective-permute-start.10 = (f32[32,16,128]{2,1,0:T(8,128)S(1)}, f32[32,16,128]{2,1,0:T(8,128)S(1)}, u32[]{:S(2)}, u32[]{:S(2)}) collective-permute-start(f32[32,16,128]{2,1,0:T(8,128)S(1)} %get-tuple-element.25), channel_id=1, source_target_pairs={{0,2},{1,3},{2,4},{3,5},{4,6},{5,7},{6,0},{7,1},{8,10},{9,11},{10,... | collective-permute-start | bytes 786440 | tf_op jit(solution)/shard_map/ppermute | solution.py:345
  95.8 52.2 %slice-start = ((s8[6291456]{0:T(1024)(128)(4,1)}), s8[4194304]{0:T(1024)(128)(4,1)S(1)}, s32[]{:S(2)}) async-start(s8[6291456]{0:T(1024)(128)(4,1)} %bitcast.14), calls=%async_computation.2 | async-start | bytes 8388608
  95.9 7.2 %collective-permute-start.12 = (f32[32,16,128]{2,1,0:T(8,128)S(1)}, f32[32,16,128]{2,1,0:T(8,128)S(1)}, u32[]{:S(2)}, u32[]{:S(2)}) collective-permute-start(f32[32,16,128]{2,1,0:T(8,128)S(1)} %get-tuple-element.36), channel_id=1, source_target_pairs={{0,6},{1,7},{2,0},{3,1},{4,2},{5,3},{6,4},{7,5},{8,14},{9,15},{10,... | collective-permute-start | bytes 786440 | tf_op jit(solution)/shard_map/ppermute | solution.py:345
  99.2 6.9 %collective-permute-start.9 = (bf16[16,16,128]{2,1,0:T(8,128)(2,1)S(1)}, bf16[16,16,128]{2,1,0:T(8,128)(2,1)S(1)}, u32[]{:S(2)}, u32[]{:S(2)}) collective-permute-start(bf16[16,16,128]{2,1,0:T(8,128)(2,1)S(1)} %get-tuple-element.46), channel_id=1, source_target_pairs={{0,8},{8,0},{16,24},{24,16},{32,40},{40,32},{48,56},{56,48},{64,72... | collective-permute-start | bytes 196616 | tf_op jit(solution)/shard_map/ppermute | solution.py:349
  103.2 5.4 %collective-permute-start.13 = (bf16[16,16,128]{2,1,0:T(8,128)(2,1)S(1)}, bf16[16,16,128]{2,1,0:T(8,128)(2,1)S(1)}, u32[]{:S(2)}, u32[]{:S(2)}) collective-permute-start(bf16[16,16,128]{2,1,0:T(8,128)(2,1)S(1)} %get-tuple-element.47), channel_id=1, source_target_pairs={{0,16},{8,24},{16,0},{24,8},{32,48},{40,56},{48,32},{56,40},{64,80... | collective-permute-start | bytes 196616 | tf_op jit(solution)/shard_map/ppermute | solution.py:349
  103.9 6.6 %collective-permute-start.14 = (bf16[16,16,128]{2,1,0:T(8,128)(2,1)S(1)}, bf16[16,16,128]{2,1,0:T(8,128)(2,1)S(1)}, u32[]{:S(2)}, u32[]{:S(2)}) collective-permute-start(bf16[16,16,128]{2,1,0:T(8,128)(2,1)S(1)} %get-tuple-element.48), channel_id=1, source_target_pairs={{0,24},{8,16},{16,8},{24,0},{32,56},{40,48},{48,40},{56,32},{64,88... | collective-permute-start | bytes 196616 | tf_op jit(solution)/shard_map/ppermute | solution.py:349
  110.5 11.7 %collective-permute-start.15 = (bf16[4,16,16,128]{3,2,1,0:T(8,128)(2,1)S(1)}, bf16[4,16,16,128]{3,2,1,0:T(8,128)(2,1)S(1)}, u32[]{:S(2)}, u32[]{:S(2)}) collective-permute-start(bf16[4,16,16,128]{3,2,1,0:T(8,128)(2,1)S(1)} %pad_maximum_fusion.1), channel_id=1, source_target_pairs={{4,0},{60,1},{64,2},{120,3},{132,4},{188,5},{192,6},{248,7},{12,8}... | collective-permute-start | bytes 786440 | tf_op jit(solution)/shard_map/ppermute | solution.py:388
  126.3 1.5 collective-permute-start.16
  127.8 6.3 %collective-permute-start.17 = (f32[2,8,1536]{2,1,0:T(8,128)S(1)}, f32[2,8,1536]{2,1,0:T(8,128)S(1)}, u32[]{:S(2)}, u32[]{:S(2)}) collective-permute-start(f32[2,8,1536]{2,1,0:T(8,128)S(1)} %slice.140), channel_id=1, source_target_pairs={{0,2},{1,3},{2,0},{3,1},{4,6},{5,7},{6,4},{7,5},{8,10},{9,11},{10,... | collective-permute-start | bytes 294920 | tf_op jit(solution)/shard_map/ppermute | solution.py:353
  134.1 7.0 %collective-permute-start.18 = (f32[1,8,1536]{2,1,0:T(8,128)S(1)}, f32[1,8,1536]{2,1,0:T(8,128)S(1)}, u32[]{:S(2)}, u32[]{:S(2)}) collective-permute-start(f32[1,8,1536]{2,1,0:T(8,128)S(1)} %slice.142), channel_id=1, source_target_pairs={{0,4},{1,5},{2,6},{3,7},{4,0},{5,1},{6,2},{7,3},{8,12},{9,13},{10,... | collective-permute-start | bytes 147464 | tf_op jit(solution)/shard_map/ppermute | solution.py:353
  141.2 4.2 %collective-permute-start.19 = (f32[1,8,1536]{2,1,0:T(8,128)S(1)}, f32[1,8,1536]{2,1,0:T(8,128)S(1)}, u32[]{:S(2)}, u32[]{:S(2)}) collective-permute-start(f32[1,8,1536]{2,1,0:T(8,128)S(1)} %slice_add_fusion.9), channel_id=1, source_target_pairs={{0,8},{8,0},{16,24},{24,16},{32,40},{40,32},{48,56},{56,48},{64,72... | collective-permute-start | bytes 147464 | tf_op jit(solution)/shard_map/ppermute | solution.py:402
  145.3 7.9 %collective-permute-start.20 = (f32[1,8,1536]{2,1,0:T(8,128)S(1)}, f32[1,8,1536]{2,1,0:T(8,128)S(1)}, u32[]{:S(2)}, u32[]{:S(2)}) collective-permute-start(f32[1,8,1536]{2,1,0:T(8,128)S(1)} %add.192), channel_id=1, source_target_pairs={{0,16},{8,24},{16,0},{24,8},{32,48},{40,56},{48,32},{56,40},{64,80... | collective-permute-start | bytes 147464 | tf_op jit(solution)/shard_map/ppermute | solution.py:402
  153.3 8.1 %collective-permute-start.21 = (f32[1,8,1536]{2,1,0:T(8,128)S(1)}, f32[1,8,1536]{2,1,0:T(8,128)S(1)}, u32[]{:S(2)}, u32[]{:S(2)}) collective-permute-start(f32[1,8,1536]{2,1,0:T(8,128)S(1)} %add.193), channel_id=1, source_target_pairs={{0,32},{8,40},{16,48},{24,56},{32,0},{40,8},{48,16},{56,24},{64,96... | collective-permute-start | bytes 147464 | tf_op jit(solution)/shard_map/ppermute | solution.py:402
  159.1 16.5 %collective-permute-start.27 = (f32[16,2,1536]{2,1,0:T(2,128)S(1)}, f32[16,2,1536]{2,1,0:T(2,128)S(1)}, u32[]{:S(2)}, u32[]{:S(2)}) collective-permute-start(f32[16,2,1536]{2,1,0:T(2,128)S(1)} %get-tuple-element.34), channel_id=1, source_target_pairs={{0,1},{1,0},{2,3},{3,2},{4,5},{5,4},{6,7},{7,6},{8,9},{9,8},{10,11... | collective-permute-start | bytes 589832 | tf_op jit(solution)/shard_map/ppermute | solution.py:353
  161.4 4.2 %collective-permute-start.22 = (f32[1,8,1536]{2,1,0:T(8,128)S(1)}, f32[1,8,1536]{2,1,0:T(8,128)S(1)}, u32[]{:S(2)}, u32[]{:S(2)}) collective-permute-start(f32[1,8,1536]{2,1,0:T(8,128)S(1)} %add.194), channel_id=1, source_target_pairs={{0,64},{8,72},{16,80},{24,88},{32,96},{40,104},{48,112},{56,120},{... | collective-permute-start | bytes 147464 | tf_op jit(solution)/shard_map/ppermute | solution.py:402
  165.6 6.1 %collective-permute-start.23 = (f32[1,8,1536]{2,1,0:T(8,128)S(1)}, f32[1,8,1536]{2,1,0:T(8,128)S(1)}, u32[]{:S(2)}, u32[]{:S(2)}) collective-permute-start(f32[1,8,1536]{2,1,0:T(8,128)S(1)} %add.195), channel_id=1, source_target_pairs={{0,128},{8,136},{16,144},{24,152},{32,160},{40,168},{48,176},{56,1... | collective-permute-start | bytes 147464 | tf_op jit(solution)/shard_map/ppermute | solution.py:402
  171.7 6.1 %collective-permute-start.24 = (f32[1,8,1536]{2,1,0:T(8,128)S(1)}, f32[1,8,1536]{2,1,0:T(8,128)S(1)}, u32[]{:S(2)}, u32[]{:S(2)}) collective-permute-start(f32[1,8,1536]{2,1,0:T(8,128)S(1)} %add.196.refs_0_), channel_id=1, source_target_pairs={{0,4},{1,5},{2,6},{3,7},{4,0},{5,1},{6,2},{7,3},{8,12},{9,13},{10,... | collective-permute-start | bytes 147464 | tf_op jit(solution)/shard_map/ppermute | solution.py:353
  175.6 7.1 %collective-permute-start.28 = (f32[16,2,1536]{2,1,0:T(2,128)S(1)}, f32[16,2,1536]{2,1,0:T(2,128)S(1)}, u32[]{:S(2)}, u32[]{:S(2)}) collective-permute-start(f32[16,2,1536]{2,1,0:T(2,128)S(1)} %add.197), channel_id=1, source_target_pairs={{0,2},{1,3},{2,0},{3,1},{4,6},{5,7},{6,4},{7,5},{8,10},{9,11},{10,... | collective-permute-start | bytes 589832 | tf_op jit(solution)/shard_map/ppermute | solution.py:353
  177.8 5.9 %collective-permute-start.25 = (f32[2,8,1536]{2,1,0:T(8,128)S(1)}, f32[2,8,1536]{2,1,0:T(8,128)S(1)}, u32[]{:S(2)}, u32[]{:S(2)}) collective-permute-start(f32[2,8,1536]{2,1,0:T(8,128)S(1)} %pad_maximum_fusion.3), channel_id=1, source_target_pairs={{0,2},{1,3},{2,0},{3,1},{4,6},{5,7},{6,4},{7,5},{8,10},{9,11},{10,... | collective-permute-start | bytes 294920 | tf_op jit(solution)/shard_map/ppermute | solution.py:353
  182.8 7.3 %collective-permute-start.29 = (f32[16,2,1536]{2,1,0:T(2,128)S(1)}, f32[16,2,1536]{2,1,0:T(2,128)S(1)}, u32[]{:S(2)}, u32[]{:S(2)}) collective-permute-start(f32[16,2,1536]{2,1,0:T(2,128)S(1)} %add.198), channel_id=1, source_target_pairs={{0,4},{1,5},{2,6},{3,7},{4,0},{5,1},{6,2},{7,3},{8,12},{9,13},{10,... | collective-permute-start | bytes 589832 | tf_op jit(solution)/shard_map/ppermute | solution.py:353
  183.8 7.1 %collective-permute-start.26 = (f32[4,8,1536]{2,1,0:T(8,128)S(1)}, f32[4,8,1536]{2,1,0:T(8,128)S(1)}, u32[]{:S(2)}, u32[]{:S(2)}) collective-permute-start(f32[4,8,1536]{2,1,0:T(8,128)S(1)} %pad_maximum_fusion.2), channel_id=1, source_target_pairs={{0,1},{1,0},{2,3},{3,2},{4,5},{5,4},{6,7},{7,6},{8,9},{9,8},{10,11... | collective-permute-start | bytes 589832 | tf_op jit(solution)/shard_map/ppermute | solution.py:353
  (9 other events, 291.9 us)
where the time goes:
time: 192 us
  waiting for transfers between devices  71.6 us (37%)
  starting transfers between devices  49.9 us (26%)
  blocking collectives  36.8 us (19%)
  Pallas kernels  30.5 us (16%)
    ppermute x11, waiting for transfers between devices, eval_flip(): return lax.ppermute(value, 'eval', [(i, i ^ bit) for i in range(NEV)])  23.3 us
    all_to_all x1, blocking collectives, swap4(): lax.all_to_all(value, axis, split_axis=0, concat_axis=0, tiled=True, axis...  20.8 us
    ppermute x11, starting transfers between devices, eval_flip(): return lax.ppermute(value, 'eval', [(i, i ^ bit) for i in range(NEV)])  17 us
    all_to_all x1, blocking collectives, per_device(): totals = lax.all_to_all(sums, 'tm', split_axis=0, concat_axis=0, tiled=True)  16 us
    ppermute x6, waiting for transfers between devices, x_step(): lax.ppermute(value, 'eval', [(i, (i + 2 * steps) % NEV) for i in range(NE...  13.8 us
    pallas_call x1, Pallas kernels, forward(): pl.pallas_call(forward_kernel, grid=(FD // FG,), in_specs=[pl.BlockSpec((...  11.7 us
    ppermute x5, waiting for transfers between devices, per_device(): moved = lax.ppermute(head, 'tm', [(i, i ^ bit) for i in range(NTM)])  11.3 us
    pallas_call x2, Pallas kernels, hidden_part(): pl.pallas_call(hidden_kernel, grid=(count,), in_specs=[pl.BlockSpec((G, T...  10.5 us
  transfers between devices with their start and end apart: 30, of which 23 were waited for; matrix products, arithmetic and copies ran while one was open for 1% of the time, Pallas kernels for 5%

commit v1 on v0

--- a/solution.py
+++ b/solution.py
@@ -23,7 +23,7 @@
 G = 2
 ROW = 16
 BROW = 32
-PARTS = 2
+PARTS = 4
 NW = 8
 HEAD_ROWS = OUT // NEV
 
@@ -380,8 +380,9 @@
     behind = x_step(four[1], -1)
     ahead_direct = x_step(four[2], 1)
     behind_direct = x_step(four[3], -1)
-    ahead = x_step(lax.optimization_barrier(half(2) + ahead), 1)
-    behind = x_step(lax.optimization_barrier(half(7) + behind), -1)
+    onward = lax.optimization_barrier((half(2) + ahead, half(7) + behind))
+    ahead = x_step(onward[0], 1)
+    behind = x_step(onward[1], -1)
     mine = [half(0) + behind_direct + ahead, half(1) + ahead_direct + behind]
     mine = jnp.concatenate(mine, axis=0).astype(BF16).reshape(4, FD, C, BLK)
     back = jnp.stack(near(mine), axis=0)

time: 192 us -> 193 us (level)
  the two profiles are of different devices: /device:TPU:34 before, /device:TPU:1 now
where the time goes in v1:
time: 193 us; the launch traced here: 190 us
  starting transfers between devices  63.9 us (33%)
  waiting for transfers between devices  58.6 us (30%)
  Pallas kernels  32.6 us (17%)
  blocking collectives  32.1 us (17%)
    ppermute x11, starting transfers between devices, eval_flip(): return lax.ppermute(value, 'eval', [(i, i ^ bit) for i in range(NEV)])  31.3 us
    all_to_all x1, blocking collectives, swap4(): lax.all_to_all(value, axis, split_axis=0, concat_axis=0, tiled=True, axis...  19.2 us
    ppermute x11, waiting for transfers between devices, eval_flip(): return lax.ppermute(value, 'eval', [(i, i ^ bit) for i in range(NEV)])  16.2 us
    all_to_all x1, blocking collectives, per_device(): totals = lax.all_to_all(sums, 'tm', split_axis=0, concat_axis=0, tiled=True)  12.9 us
    ppermute x6, waiting for transfers between devices, x_step(): lax.ppermute(value, 'eval', [(i, (i + 2 * steps) % NEV) for i in range(NE...  12.7 us
    pallas_call x4, Pallas kernels, hidden_part(): pl.pallas_call(hidden_kernel, grid=(count,), in_specs=[pl.BlockSpec((G, T...  12.6 us
    pallas_call x1, Pallas kernels, forward(): pl.pallas_call(forward_kernel, grid=(FD // FG,), in_specs=[pl.BlockSpec((...  11.7 us
    ppermute x1, starting transfers between devices, per_device(): lax.ppermute(pieces, both, far_pairs())  9.41 us
  transfers between devices with their start and end apart: 30, of which 22 were waited for; matrix products, arithmetic and copies ran while one was open for 1% of the time, Pallas kernels for 7%

profile of v1, /device:TPU:1, one launch (start us, length us, event | category | flops | bytes accessed | tf_op | source)
XLA Modules:
  0.0 190.1 jit_solution(11055714684423213706)
XLA Ops:
  0.6 11.7 %forward.1 = (bf16[16,128,1536]{2,1,0:T(8,128)(2,1)}, f32[16,128,128]{2,1,0:T(8,128)}, bf16[4,16,16,128]{3,2,1,0:T(8,128)(2,1)}) custom-call(bf16[16,128,1536]{2,1,0:T(8,128)(2,1)} %x_ref.9, f32[16,2,1536]{2,1,0:T(2,128)} %mod_ref.9, bf16[64,1536]{1,0:T(8,128)(2,1)} %w_ref.9), custom_call_target="tpu_custom_call" | custom-call | tf_op jit(solution)/shard_map/forward/pallas_call | solution.py:89
  12.4 9.4 %collective-permute-start = (bf16[4,16,16,128]{3,2,1,0:T(8,128)(2,1)}, bf16[4,16,16,128]{3,2,1,0:T(8,128)(2,1)S(1)}, u32[]{:S(2)}, u32[]{:S(2)}) collective-permute-start(bf16[4,16,16,128]{3,2,1,0:T(8,128)(2,1)} %get-tuple-element.26), channel_id=1, source_target_pairs={{0,4},{1,60},{2,64},{3,120},{4,132},{5,188},{6,192},{7,248},{8,12}... | collective-permute-start | bytes 786440 | tf_op jit(solution)/shard_map/ppermute | solution.py:367
  21.8 7.2 %collective-permute-done = bf16[4,16,16,128]{3,2,1,0:T(8,128)(2,1)S(1)} collective-permute-done((bf16[4,16,16,128]{3,2,1,0:T(8,128)(2,1)}, bf16[4,16,16,128]{3,2,1,0:T(8,128)(2,1)S(1)}, u32[]{:S(2)}, u32[]{:S(2)}) %collective-permute-start) | collective-permute-done | bytes 262176 | tf_op jit(solution)/shard_map/ppermute | solution.py:367
  30.8 1.9 %collective-permute-start.1 = (bf16[16,16,128]{2,1,0:T(8,128)(2,1)S(1)}, bf16[16,16,128]{2,1,0:T(8,128)(2,1)S(1)}, u32[]{:S(2)}, u32[]{:S(2)}) collective-permute-start(bf16[16,16,128]{2,1,0:T(8,128)(2,1)S(1)} %get-tuple-element.58), channel_id=1, source_target_pairs={{0,8},{8,0},{16,24},{24,16},{32,40},{40,32},{48,56},{56,48},{64,72... | collective-permute-start | bytes 196616 | tf_op jit(solution)/shard_map/ppermute | solution.py:349
  35.7 19.2 %all_to_all.10 = bf16[4,64,16,128]{3,2,1,0:T(8,128)(2,1)S(1)} all-to-all(bf16[4,64,16,128]{3,2,1,0:T(8,128)(2,1)S(1)} %broadcast_in_dim.6), channel_id=1, replica_groups={{0,2,4,6},{1,3,5,7},{8,10,12,14},{9,11,13,15},{16,18,20,22},{17,19,21,2..., dimensions={0} | all-to-all | bytes 2097152 | tf_op jit(solution)/shard_map/all_to_all | solution.py:357
  56.1 2.2 %collective-permute-done.4.other_ref = bf16[256,16,128]{2,1,0:T(8,128)(2,1)S(1)} collective-permute-done((bf16[256,16,128]{2,1,0:T(8,128)(2,1)S(1)}, bf16[256,16,128]{2,1,0:T(8,128)(2,1)S(1)}, u32[]{:S(2)}, u32[]{:S(2)}) %collective-permute-start.4) | collective-permute-done | bytes 1048608 | tf_op jit(solution)/shard_map/ppermute | solution.py:353
  59.9 12.9 %all_to_all.11.tot_ref = f32[32,1,128]{2,1,0:T(1,128)S(1)} all-to-all(f32[32,1,128]{2,1,0:T(1,128)S(1)} %window_sums.1), channel_id=1, replica_groups=mesh['tm'=32,'eval'=8] {'tm'}, dimensions={0} | all-to-all | bytes 32768 | tf_op jit(solution)/shard_map/all_to_all | solution.py:371
  72.8 2.0 %window_grads.1 = (f32[256,16,128]{2,1,0:T(8,128)S(1)}, f32[256,16,128]{2,1,0:T(8,128)S(1)}) custom-call(s32[8,21]{1,0:T(8,128)S(1)} %get-tuple-element.64.row_ref, s32[8]{0:T(128)S(1)} %copy-done.5, f32[32,1,128]{2,1,0:T(1,128)S(1)} %all_to_all.11.tot_ref, bf16[8,21,16,128]{3,2,1,0:T(8,128)(2,1)S(1)} %copy-done.3, bf16[8,21,16,128]{3,2,1,0:T(8,128)(2,1)S(1)} %copy-done.4), custom_call_target="tpu_custom_call" | custom-call | tf_op jit(solution)/shard_map/window_grads/pallas_call | solution.py:189
  74.8 1.9 collective-permute-start.5
  76.7 3.8 %collective-permute-done.5 = f32[256,16,128]{2,1,0:T(8,128)S(1)} collective-permute-done((f32[256,16,128]{2,1,0:T(8,128)S(1)}, f32[256,16,128]{2,1,0:T(8,128)S(1)}, u32[]{:S(2)}, u32[]{:S(2)}) %collective-permute-start.5) | collective-permute-done | bytes 2097184 | tf_op jit(solution)/shard_map/ppermute | solution.py:353
  81.1 2.4 %collective-permute-start.8 = (f32[32,16,128]{2,1,0:T(8,128)S(1)}, f32[32,16,128]{2,1,0:T(8,128)S(1)}, u32[]{:S(2)}, u32[]{:S(2)}) collective-permute-start(f32[32,16,128]{2,1,0:T(8,128)S(1)} %get-tuple-element.31), channel_id=1, source_target_pairs={{0,6},{1,7},{2,0},{3,1},{4,2},{5,3},{6,4},{7,5},{8,14},{9,15},{10,... | collective-permute-start | bytes 786440 | tf_op jit(solution)/shard_map/ppermute | solution.py:345
  84.9 4.6 %collective-permute-done.7 = f32[32,16,128]{2,1,0:T(8,128)S(1)} collective-permute-done((f32[32,16,128]{2,1,0:T(8,128)S(1)}, f32[32,16,128]{2,1,0:T(8,128)S(1)}, u32[]{:S(2)}, u32[]{:S(2)}) %collective-permute-start.7) | collective-permute-done | bytes 262176 | tf_op jit(solution)/shard_map/ppermute | solution.py:345
  89.9 2.7 %collective-permute-start.12 = (f32[32,16,128]{2,1,0:T(8,128)S(1)}, f32[32,16,128]{2,1,0:T(8,128)S(1)}, u32[]{:S(2)}, u32[]{:S(2)}) collective-permute-start(f32[32,16,128]{2,1,0:T(8,128)S(1)} %get-tuple-element.34), channel_id=1, source_target_pairs={{0,6},{1,7},{2,0},{3,1},{4,2},{5,3},{6,4},{7,5},{8,14},{9,15},{10,... | collective-permute-start | bytes 786440 | tf_op jit(solution)/shard_map/ppermute | solution.py:345
  95.1 5.6 %collective-permute-done.9 = f32[32,16,128]{2,1,0:T(8,128)S(1)} collective-permute-done((f32[32,16,128]{2,1,0:T(8,128)S(1)}, f32[32,16,128]{2,1,0:T(8,128)S(1)}, u32[]{:S(2)}, u32[]{:S(2)}) %collective-permute-start.9) | collective-permute-done | bytes 262176 | tf_op jit(solution)/shard_map/ppermute | solution.py:345
  101.8 2.9 %collective-permute-start.14 = (bf16[16,16,128]{2,1,0:T(8,128)(2,1)S(1)}, bf16[16,16,128]{2,1,0:T(8,128)(2,1)S(1)}, u32[]{:S(2)}, u32[]{:S(2)}) collective-permute-start(bf16[16,16,128]{2,1,0:T(8,128)(2,1)S(1)} %get-tuple-element.62), channel_id=1, source_target_pairs={{0,24},{8,16},{16,8},{24,0},{32,56},{40,48},{48,40},{56,32},{64,88... | collective-permute-start | bytes 196616 | tf_op jit(solution)/shard_map/ppermute | solution.py:349
  105.5 1.8 collective-permute-done.14
  107.4 3.9 %collective-permute-start.15 = (bf16[4,16,16,128]{3,2,1,0:T(8,128)(2,1)S(1)}, bf16[4,16,16,128]{3,2,1,0:T(8,128)(2,1)S(1)}, u32[]{:S(2)}, u32[]{:S(2)}) collective-permute-start(bf16[4,16,16,128]{3,2,1,0:T(8,128)(2,1)S(1)} %pad_maximum_fusion.1), channel_id=1, source_target_pairs={{4,0},{60,1},{64,2},{120,3},{132,4},{188,5},{192,6},{248,7},{12,8}... | collective-permute-start | bytes 786440 | tf_op jit(solution)/shard_map/ppermute | solution.py:389
  111.3 8.4 %collective-permute-done.15.g_ref = bf16[4,16,16,128]{3,2,1,0:T(8,128)(2,1)S(1)} collective-permute-done((bf16[4,16,16,128]{3,2,1,0:T(8,128)(2,1)S(1)}, bf16[4,16,16,128]{3,2,1,0:T(8,128)(2,1)S(1)}, u32[]{:S(2)}, u32[]{:S(2)}) %collective-permute-start.15) | collective-permute-done | bytes 262176 | tf_op jit(solution)/shard_map/ppermute | solution.py:389
  119.7 3.9 %head_part.1 = (bf16[16,64,128]{2,1,0:T(8,128)(2,1)S(1)}, f32[4,8,1536]{2,1,0:T(8,128)S(1)}, f32[4,8,1536]{2,1,0:T(8,128)S(1)}) custom-call(bf16[4,16,16,128]{3,2,1,0:T(8,128)(2,1)S(1)} %collective-permute-done.15.g_ref, bf16[16,128,1536]{2,1,0:T(8,128)(2,1)S(1)} %bitcast.17), custom_call_target="tpu_custom_call" | custom-call | tf_op jit(solution)/shard_map/head_part/pallas_call | solution.py:235
  123.7 3.7 %collective-permute-start.16 = (f32[4,8,1536]{2,1,0:T(8,128)S(1)}, f32[4,8,1536]{2,1,0:T(8,128)S(1)}, u32[]{:S(2)}, u32[]{:S(2)}) collective-permute-start(f32[4,8,1536]{2,1,0:T(8,128)S(1)} %get-tuple-element.45), channel_id=1, source_target_pairs={{0,1},{1,0},{2,3},{3,2},{4,5},{5,4},{6,7},{7,6},{8,9},{9,8},{10,11... | collective-permute-start | bytes 589832 | tf_op jit(solution)/shard_map/ppermute | solution.py:353
  128.6 4.0 %collective-permute-done.17 = f32[2,8,1536]{2,1,0:T(8,128)S(1)} collective-permute-done((f32[2,8,1536]{2,1,0:T(8,128)S(1)}, f32[2,8,1536]{2,1,0:T(8,128)S(1)}, u32[]{:S(2)}, u32[]{:S(2)}) %collective-permute-start.17) | collective-permute-done | bytes 98336 | tf_op jit(solution)/shard_map/ppermute | solution.py:353
  132.5 6.3 %collective-permute-start.18 = (f32[1,8,1536]{2,1,0:T(8,128)S(1)}, f32[1,8,1536]{2,1,0:T(8,128)S(1)}, u32[]{:S(2)}, u32[]{:S(2)}) collective-permute-start(f32[1,8,1536]{2,1,0:T(8,128)S(1)} %slice.142), channel_id=1, source_target_pairs={{0,4},{1,5},{2,6},{3,7},{4,0},{5,1},{6,2},{7,3},{8,12},{9,13},{10,... | collective-permute-start | bytes 147464 | tf_op jit(solution)/shard_map/ppermute | solution.py:353
  144.9 3.1 %hidden_part.4 = (bf16[16,128,1536]{2,1,0:T(8,128)(2,1)}, f32[16,2,1536]{2,1,0:T(2,128)S(1)}) custom-call(bf16[16,128,1536]{2,1,0:T(8,128)(2,1)S(1)} %bitcast.15, f32[16,128,128]{2,1,0:T(8,128)S(1)} %copy-done, bf16[16,64,128]{2,1,0:T(8,128)(2,1)S(1)} %get-tuple-element.36.up_ref, f32[16,2,1536]{2,1,0:T(2,128)S(1)} %copy-done.1, bf16[64,1536]{1,0:T(8,128)(2,1)S(1)} %copy-done.2), custom_call_target="tpu_custom_call" | custom-call | flops 31457280 | bytes 3932160 | tf_op jit(solution)/shard_map/hidden_part/pallas_call | solution.py:283
  148.1 3.1 %hidden_part.5 = (bf16[16,128,1536]{2,1,0:T(8,128)(2,1)}, f32[16,2,1536]{2,1,0:T(2,128)S(1)}) custom-call(bf16[16,128,1536]{2,1,0:T(8,128)(2,1)S(1)} %bitcast.15, f32[16,128,128]{2,1,0:T(8,128)S(1)} %copy-done, bf16[16,64,128]{2,1,0:T(8,128)(2,1)S(1)} %get-tuple-element.36.up_ref, ...), custom_call_target="tpu_custom_call", output_to_operand_aliasing={{0}: (5, {}), {1}: (6, {})} | custom-call | flops 31457280 | bytes 3932160 | tf_op jit(solution)/shard_map/hidden_part/pallas_call | solution.py:283
  151.2 3.1 %hidden_part.6 = (bf16[16,128,1536]{2,1,0:T(8,128)(2,1)}, f32[16,2,1536]{2,1,0:T(2,128)S(1)}) custom-call(bf16[16,128,1536]{2,1,0:T(8,128)(2,1)S(1)} %bitcast.15, f32[16,128,128]{2,1,0:T(8,128)S(1)} %copy-done, bf16[16,64,128]{2,1,0:T(8,128)(2,1)S(1)} %get-tuple-element.36.up_ref, ...), custom_call_target="tpu_custom_call", output_to_operand_aliasing={{0}: (5, {}), {1}: (6, {})} | custom-call | flops 31457280 | bytes 3932160 | tf_op jit(solution)/shard_map/hidden_part/pallas_call | solution.py:283
  154.7 3.2 %hidden_part.7 = (bf16[16,128,1536]{2,1,0:T(8,128)(2,1)}, f32[16,2,1536]{2,1,0:T(2,128)S(1)}) custom-call(bf16[16,128,1536]{2,1,0:T(8,128)(2,1)S(1)} %bitcast.15, f32[16,128,128]{2,1,0:T(8,128)S(1)} %copy-done, bf16[16,64,128]{2,1,0:T(8,128)(2,1)S(1)} %get-tuple-element.36.up_ref, ...), custom_call_target="tpu_custom_call", output_to_operand_aliasing={{0}: (5, {}), {1}: (6, {})} | custom-call | flops 31457280 | bytes 3932160 | tf_op jit(solution)/shard_map/hidden_part/pallas_call | solution.py:283
  157.8 3.4 %collective-permute-start.27 = (f32[16,2,1536]{2,1,0:T(2,128)S(1)}, f32[16,2,1536]{2,1,0:T(2,128)S(1)}, u32[]{:S(2)}, u32[]{:S(2)}) collective-permute-start(f32[16,2,1536]{2,1,0:T(2,128)S(1)} %get-tuple-element.46), channel_id=1, source_target_pairs={{0,1},{1,0},{2,3},{3,2},{4,5},{5,4},{6,7},{7,6},{8,9},{9,8},{10,11... | collective-permute-start | bytes 589832 | tf_op jit(solution)/shard_map/ppermute | solution.py:353
  162.0 3.2 %collective-permute-done.22 = f32[1,8,1536]{2,1,0:T(8,128)S(1)} collective-permute-done((f32[1,8,1536]{2,1,0:T(8,128)S(1)}, f32[1,8,1536]{2,1,0:T(8,128)S(1)}, u32[]{:S(2)}, u32[]{:S(2)}) %collective-permute-start.22) | collective-permute-done | bytes 49184 | tf_op jit(solution)/shard_map/ppermute | solution.py:403
  166.9 2.9 %collective-permute-done.23 = f32[1,8,1536]{2,1,0:T(8,128)S(1)} collective-permute-done((f32[1,8,1536]{2,1,0:T(8,128)S(1)}, f32[1,8,1536]{2,1,0:T(8,128)S(1)}, u32[]{:S(2)}, u32[]{:S(2)}) %collective-permute-start.23) | collective-permute-done | bytes 49184 | tf_op jit(solution)/shard_map/ppermute | solution.py:403
  169.8 3.1 %collective-permute-start.24 = (f32[1,8,1536]{2,1,0:T(8,128)S(1)}, f32[1,8,1536]{2,1,0:T(8,128)S(1)}, u32[]{:S(2)}, u32[]{:S(2)}) collective-permute-start(f32[1,8,1536]{2,1,0:T(8,128)S(1)} %add.196.refs_0_), channel_id=1, source_target_pairs={{0,4},{1,5},{2,6},{3,7},{4,0},{5,1},{6,2},{7,3},{8,12},{9,13},{10,... | collective-permute-start | bytes 147464 | tf_op jit(solution)/shard_map/ppermute | solution.py:353
  175.0 2.6 %collective-permute-done.28 = f32[16,2,1536]{2,1,0:T(2,128)S(1)} collective-permute-done((f32[16,2,1536]{2,1,0:T(2,128)S(1)}, f32[16,2,1536]{2,1,0:T(2,128)S(1)}, u32[]{:S(2)}, u32[]{:S(2)}) %collective-permute-start.28) | collective-permute-done | bytes 196640 | tf_op jit(solution)/shard_map/ppermute | solution.py:353
  178.8 9.4 %collective-permute-start.26 = (f32[4,8,1536]{2,1,0:T(8,128)S(1)}, f32[4,8,1536]{2,1,0:T(8,128)S(1)}, u32[]{:S(2)}, u32[]{:S(2)}) collective-permute-start(f32[4,8,1536]{2,1,0:T(8,128)S(1)} %pad_maximum_fusion.2), channel_id=1, source_target_pairs={{0,1},{1,0},{2,3},{3,2},{4,5},{5,4},{6,7},{7,6},{8,9},{9,8},{10,11... | collective-permute-start | bytes 589832 | tf_op jit(solution)/shard_map/ppermute | solution.py:353
  (88 shorter events, 29.4 us)
Async XLA Ops:
  12.4 16.7 %collective-permute-start = (bf16[4,16,16,128]{3,2,1,0:T(8,128)(2,1)}, bf16[4,16,16,128]{3,2,1,0:T(8,128)(2,1)S(1)}, u32[]{:S(2)}, u32[]{:S(2)}) collective-permute-start(bf16[4,16,16,128]{3,2,1,0:T(8,128)(2,1)} %get-tuple-element.26), channel_id=1, source_target_pairs={{0,4},{1,60},{2,64},{3,120},{4,132},{5,188},{6,192},{7,248},{8,12}... | collective-permute-start | bytes 786440 | tf_op jit(solution)/shard_map/ppermute | solution.py:367
  29.1 5.0 %collective-permute-start.3 = (bf16[16,16,128]{2,1,0:T(8,128)(2,1)S(1)}, bf16[16,16,128]{2,1,0:T(8,128)(2,1)S(1)}, u32[]{:S(2)}, u32[]{:S(2)}) collective-permute-start(bf16[16,16,128]{2,1,0:T(8,128)(2,1)S(1)} %get-tuple-element.56), channel_id=1, source_target_pairs={{0,24},{8,16},{16,8},{24,0},{32,56},{40,48},{48,40},{56,32},{64,88... | collective-permute-start | bytes 196616 | tf_op jit(solution)/shard_map/ppermute | solution.py:349
  30.8 4.7 %collective-permute-start.2 = (bf16[16,16,128]{2,1,0:T(8,128)(2,1)S(1)}, bf16[16,16,128]{2,1,0:T(8,128)(2,1)S(1)}, u32[]{:S(2)}, u32[]{:S(2)}) collective-permute-start(bf16[16,16,128]{2,1,0:T(8,128)(2,1)S(1)} %get-tuple-element.57), channel_id=1, source_target_pairs={{0,16},{8,24},{16,0},{24,8},{32,48},{40,56},{48,32},{56,40},{64,80... | collective-permute-start | bytes 196616 | tf_op jit(solution)/shard_map/ppermute | solution.py:349
  30.8 4.7 %collective-permute-start.1 = (bf16[16,16,128]{2,1,0:T(8,128)(2,1)S(1)}, bf16[16,16,128]{2,1,0:T(8,128)(2,1)S(1)}, u32[]{:S(2)}, u32[]{:S(2)}) collective-permute-start(bf16[16,16,128]{2,1,0:T(8,128)(2,1)S(1)} %get-tuple-element.58), channel_id=1, source_target_pairs={{0,8},{8,0},{16,24},{24,16},{32,40},{40,32},{48,56},{56,48},{64,72... | collective-permute-start | bytes 196616 | tf_op jit(solution)/shard_map/ppermute | solution.py:349
  54.9 3.4 %collective-permute-start.4 = (bf16[256,16,128]{2,1,0:T(8,128)(2,1)S(1)}, bf16[256,16,128]{2,1,0:T(8,128)(2,1)S(1)}, u32[]{:S(2)}, u32[]{:S(2)}) collective-permute-start(bf16[256,16,128]{2,1,0:T(8,128)(2,1)S(1)} %bitcast.18), channel_id=1, source_target_pairs={{0,1},{1,0},{2,3},{3,2},{4,5},{5,4},{6,7},{7,6},{8,9},{9,8},{10,11... | collective-permute-start | bytes 3145736 | tf_op jit(solution)/shard_map/ppermute | solution.py:353
  58.3 61.4 %slice-start.2 = ((s8[6291456]{0:T(1024)(128)(4,1)}), s8[2097152]{0:T(1024)(128)(4,1)S(1)}, s32[]{:S(2)}) async-start(s8[6291456]{0:T(1024)(128)(4,1)} %bitcast.16), calls=%async_computation.4 | async-start | bytes 4194304
  74.8 5.7 %collective-permute-start.5 = (f32[256,16,128]{2,1,0:T(8,128)S(1)}, f32[256,16,128]{2,1,0:T(8,128)S(1)}, u32[]{:S(2)}, u32[]{:S(2)}) collective-permute-start(f32[256,16,128]{2,1,0:T(8,128)S(1)} %get-tuple-element.28), channel_id=1, source_target_pairs={{0,1},{1,0},{2,3},{3,2},{4,5},{5,4},{6,7},{7,6},{8,9},{9,8},{10,11... | collective-permute-start | bytes 6291464 | tf_op jit(solution)/shard_map/ppermute | solution.py:353
  80.7 8.8 %collective-permute-start.7 = (f32[32,16,128]{2,1,0:T(8,128)S(1)}, f32[32,16,128]{2,1,0:T(8,128)S(1)}, u32[]{:S(2)}, u32[]{:S(2)}) collective-permute-start(f32[32,16,128]{2,1,0:T(8,128)S(1)} %get-tuple-element.30), channel_id=1, source_target_pairs={{0,2},{1,3},{2,4},{3,5},{4,6},{5,7},{6,0},{7,1},{8,10},{9,11},{10,... | collective-permute-start | bytes 786440 | tf_op jit(solution)/shard_map/ppermute | solution.py:345
  81.1 8.4 %collective-permute-start.8 = (f32[32,16,128]{2,1,0:T(8,128)S(1)}, f32[32,16,128]{2,1,0:T(8,128)S(1)}, u32[]{:S(2)}, u32[]{:S(2)}) collective-permute-start(f32[32,16,128]{2,1,0:T(8,128)S(1)} %get-tuple-element.31), channel_id=1, source_target_pairs={{0,6},{1,7},{2,0},{3,1},{4,2},{5,3},{6,4},{7,5},{8,14},{9,15},{10,... | collective-permute-start | bytes 786440 | tf_op jit(solution)/shard_map/ppermute | solution.py:345
  83.5 10.6 %collective-permute-start.6 = (f32[32,16,128]{2,1,0:T(8,128)S(1)}, f32[32,16,128]{2,1,0:T(8,128)S(1)}, u32[]{:S(2)}, u32[]{:S(2)}) collective-permute-start(f32[32,16,128]{2,1,0:T(8,128)S(1)} %get-tuple-element.29), channel_id=1, source_target_pairs={{0,6},{1,7},{2,0},{3,1},{4,2},{5,3},{6,4},{7,5},{8,14},{9,15},{10,... | collective-permute-start | bytes 786440 | tf_op jit(solution)/shard_map/ppermute | solution.py:345
  83.5 11.6 %collective-permute-start.11 = (f32[32,16,128]{2,1,0:T(8,128)S(1)}, f32[32,16,128]{2,1,0:T(8,128)S(1)}, u32[]{:S(2)}, u32[]{:S(2)}) collective-permute-start(f32[32,16,128]{2,1,0:T(8,128)S(1)} %get-tuple-element.33), channel_id=1, source_target_pairs={{0,2},{1,3},{2,4},{3,5},{4,6},{5,7},{6,0},{7,1},{8,10},{9,11},{10,... | collective-permute-start | bytes 786440 | tf_op jit(solution)/shard_map/ppermute | solution.py:345
  89.6 11.1 %collective-permute-start.9 = (f32[32,16,128]{2,1,0:T(8,128)S(1)}, f32[32,16,128]{2,1,0:T(8,128)S(1)}, u32[]{:S(2)}, u32[]{:S(2)}) collective-permute-start(f32[32,16,128]{2,1,0:T(8,128)S(1)} %get-tuple-element.32), channel_id=1, source_target_pairs={{0,2},{1,3},{2,4},{3,5},{4,6},{5,7},{6,0},{7,1},{8,10},{9,11},{10,... | collective-permute-start | bytes 786440 | tf_op jit(solution)/shard_map/ppermute | solution.py:345
  89.9 10.8 %collective-permute-start.12 = (f32[32,16,128]{2,1,0:T(8,128)S(1)}, f32[32,16,128]{2,1,0:T(8,128)S(1)}, u32[]{:S(2)}, u32[]{:S(2)}) collective-permute-start(f32[32,16,128]{2,1,0:T(8,128)S(1)} %get-tuple-element.34), channel_id=1, source_target_pairs={{0,6},{1,7},{2,0},{3,1},{4,2},{5,3},{6,4},{7,5},{8,14},{9,15},{10,... | collective-permute-start | bytes 786440 | tf_op jit(solution)/shard_map/ppermute | solution.py:345
  100.7 44.2 %slice-start = ((s8[6291456]{0:T(1024)(128)(4,1)}), s8[4194304]{0:T(1024)(128)(4,1)S(1)}, s32[]{:S(2)}) async-start(s8[6291456]{0:T(1024)(128)(4,1)} %bitcast.14), calls=%async_computation.2 | async-start | bytes 8388608
  100.9 3.7 %collective-permute-start.10 = (bf16[16,16,128]{2,1,0:T(8,128)(2,1)S(1)}, bf16[16,16,128]{2,1,0:T(8,128)(2,1)S(1)}, u32[]{:S(2)}, u32[]{:S(2)}) collective-permute-start(bf16[16,16,128]{2,1,0:T(8,128)(2,1)S(1)} %get-tuple-element.60), channel_id=1, source_target_pairs={{0,8},{8,0},{16,24},{24,16},{32,40},{40,32},{48,56},{56,48},{64,72... | collective-permute-start | bytes 196616 | tf_op jit(solution)/shard_map/ppermute | solution.py:349
  101.4 4.1 %collective-permute-start.13 = (bf16[16,16,128]{2,1,0:T(8,128)(2,1)S(1)}, bf16[16,16,128]{2,1,0:T(8,128)(2,1)S(1)}, u32[]{:S(2)}, u32[]{:S(2)}) collective-permute-start(bf16[16,16,128]{2,1,0:T(8,128)(2,1)S(1)} %get-tuple-element.61), channel_id=1, source_target_pairs={{0,16},{8,24},{16,0},{24,8},{32,48},{40,56},{48,32},{56,40},{64,80... | collective-permute-start | bytes 196616 | tf_op jit(solution)/shard_map/ppermute | solution.py:349
  101.8 5.6 %collective-permute-start.14 = (bf16[16,16,128]{2,1,0:T(8,128)(2,1)S(1)}, bf16[16,16,128]{2,1,0:T(8,128)(2,1)S(1)}, u32[]{:S(2)}, u32[]{:S(2)}) collective-permute-start(bf16[16,16,128]{2,1,0:T(8,128)(2,1)S(1)} %get-tuple-element.62), channel_id=1, source_target_pairs={{0,24},{8,16},{16,8},{24,0},{32,56},{40,48},{48,40},{56,32},{64,88... | collective-permute-start | bytes 196616 | tf_op jit(solution)/shard_map/ppermute | solution.py:349
  107.4 12.3 %collective-permute-start.15 = (bf16[4,16,16,128]{3,2,1,0:T(8,128)(2,1)S(1)}, bf16[4,16,16,128]{3,2,1,0:T(8,128)(2,1)S(1)}, u32[]{:S(2)}, u32[]{:S(2)}) collective-permute-start(bf16[4,16,16,128]{3,2,1,0:T(8,128)(2,1)S(1)} %pad_maximum_fusion.1), channel_id=1, source_target_pairs={{4,0},{60,1},{64,2},{120,3},{132,4},{188,5},{192,6},{248,7},{12,8}... | collective-permute-start | bytes 786440 | tf_op jit(solution)/shard_map/ppermute | solution.py:389
  123.7 4.7 %collective-permute-start.16 = (f32[4,8,1536]{2,1,0:T(8,128)S(1)}, f32[4,8,1536]{2,1,0:T(8,128)S(1)}, u32[]{:S(2)}, u32[]{:S(2)}) collective-permute-start(f32[4,8,1536]{2,1,0:T(8,128)S(1)} %get-tuple-element.45), channel_id=1, source_target_pairs={{0,1},{1,0},{2,3},{3,2},{4,5},{5,4},{6,7},{7,6},{8,9},{9,8},{10,11... | collective-permute-start | bytes 589832 | tf_op jit(solution)/shard_map/ppermute | solution.py:353
  128.5 4.1 %collective-permute-start.17 = (f32[2,8,1536]{2,1,0:T(8,128)S(1)}, f32[2,8,1536]{2,1,0:T(8,128)S(1)}, u32[]{:S(2)}, u32[]{:S(2)}) collective-permute-start(f32[2,8,1536]{2,1,0:T(8,128)S(1)} %slice.140), channel_id=1, source_target_pairs={{0,2},{1,3},{2,0},{3,1},{4,6},{5,7},{6,4},{7,5},{8,10},{9,11},{10,... | collective-permute-start | bytes 294920 | tf_op jit(solution)/shard_map/ppermute | solution.py:353
  132.5 7.8 %collective-permute-start.18 = (f32[1,8,1536]{2,1,0:T(8,128)S(1)}, f32[1,8,1536]{2,1,0:T(8,128)S(1)}, u32[]{:S(2)}, u32[]{:S(2)}) collective-permute-start(f32[1,8,1536]{2,1,0:T(8,128)S(1)} %slice.142), channel_id=1, source_target_pairs={{0,4},{1,5},{2,6},{3,7},{4,0},{5,1},{6,2},{7,3},{8,12},{9,13},{10,... | collective-permute-start | bytes 147464 | tf_op jit(solution)/shard_map/ppermute | solution.py:353
  140.4 3.0 %collective-permute-start.19 = (f32[1,8,1536]{2,1,0:T(8,128)S(1)}, f32[1,8,1536]{2,1,0:T(8,128)S(1)}, u32[]{:S(2)}, u32[]{:S(2)}) collective-permute-start(f32[1,8,1536]{2,1,0:T(8,128)S(1)} %slice_add_fusion.9), channel_id=1, source_target_pairs={{0,8},{8,0},{16,24},{24,16},{32,40},{40,32},{48,56},{56,48},{64,72... | collective-permute-start | bytes 147464 | tf_op jit(solution)/shard_map/ppermute | solution.py:403
  143.4 10.9 %collective-permute-start.20 = (f32[1,8,1536]{2,1,0:T(8,128)S(1)}, f32[1,8,1536]{2,1,0:T(8,128)S(1)}, u32[]{:S(2)}, u32[]{:S(2)}) collective-permute-start(f32[1,8,1536]{2,1,0:T(8,128)S(1)} %add.192), channel_id=1, source_target_pairs={{0,16},{8,24},{16,0},{24,8},{32,48},{40,56},{48,32},{56,40},{64,80... | collective-permute-start | bytes 147464 | tf_op jit(solution)/shard_map/ppermute | solution.py:403
  154.3 7.6 %collective-permute-start.21 = (f32[1,8,1536]{2,1,0:T(8,128)S(1)}, f32[1,8,1536]{2,1,0:T(8,128)S(1)}, u32[]{:S(2)}, u32[]{:S(2)}) collective-permute-start(f32[1,8,1536]{2,1,0:T(8,128)S(1)} %add.193), channel_id=1, source_target_pairs={{0,32},{8,40},{16,48},{24,56},{32,0},{40,8},{48,16},{56,24},{64,96... | collective-permute-start | bytes 147464 | tf_op jit(solution)/shard_map/ppermute | solution.py:403
  157.8 15.1 %collective-permute-start.27 = (f32[16,2,1536]{2,1,0:T(2,128)S(1)}, f32[16,2,1536]{2,1,0:T(2,128)S(1)}, u32[]{:S(2)}, u32[]{:S(2)}) collective-permute-start(f32[16,2,1536]{2,1,0:T(2,128)S(1)} %get-tuple-element.46), channel_id=1, source_target_pairs={{0,1},{1,0},{2,3},{3,2},{4,5},{5,4},{6,7},{7,6},{8,9},{9,8},{10,11... | collective-permute-start | bytes 589832 | tf_op jit(solution)/shard_map/ppermute | solution.py:353
  161.9 3.3 %collective-permute-start.22 = (f32[1,8,1536]{2,1,0:T(8,128)S(1)}, f32[1,8,1536]{2,1,0:T(8,128)S(1)}, u32[]{:S(2)}, u32[]{:S(2)}) collective-permute-start(f32[1,8,1536]{2,1,0:T(8,128)S(1)} %add.194), channel_id=1, source_target_pairs={{0,64},{8,72},{16,80},{24,88},{32,96},{40,104},{48,112},{56,120},{... | collective-permute-start | bytes 147464 | tf_op jit(solution)/shard_map/ppermute | solution.py:403
  165.2 4.5 %collective-permute-start.23 = (f32[1,8,1536]{2,1,0:T(8,128)S(1)}, f32[1,8,1536]{2,1,0:T(8,128)S(1)}, u32[]{:S(2)}, u32[]{:S(2)}) collective-permute-start(f32[1,8,1536]{2,1,0:T(8,128)S(1)} %add.195), channel_id=1, source_target_pairs={{0,128},{8,136},{16,144},{24,152},{32,160},{40,168},{48,176},{56,1... | collective-permute-start | bytes 147464 | tf_op jit(solution)/shard_map/ppermute | solution.py:403
  169.8 4.6 %collective-permute-start.24 = (f32[1,8,1536]{2,1,0:T(8,128)S(1)}, f32[1,8,1536]{2,1,0:T(8,128)S(1)}, u32[]{:S(2)}, u32[]{:S(2)}) collective-permute-start(f32[1,8,1536]{2,1,0:T(8,128)S(1)} %add.196.refs_0_), channel_id=1, source_target_pairs={{0,4},{1,5},{2,6},{3,7},{4,0},{5,1},{6,2},{7,3},{8,12},{9,13},{10,... | collective-permute-start | bytes 147464 | tf_op jit(solution)/shard_map/ppermute | solution.py:353
  173.0 4.6 %collective-permute-start.28 = (f32[16,2,1536]{2,1,0:T(2,128)S(1)}, f32[16,2,1536]{2,1,0:T(2,128)S(1)}, u32[]{:S(2)}, u32[]{:S(2)}) collective-permute-start(f32[16,2,1536]{2,1,0:T(2,128)S(1)} %add.197), channel_id=1, source_target_pairs={{0,2},{1,3},{2,0},{3,1},{4,6},{5,7},{6,4},{7,5},{8,10},{9,11},{10,... | collective-permute-start | bytes 589832 | tf_op jit(solution)/shard_map/ppermute | solution.py:353
  174.4 4.4 %collective-permute-start.25 = (f32[2,8,1536]{2,1,0:T(8,128)S(1)}, f32[2,8,1536]{2,1,0:T(8,128)S(1)}, u32[]{:S(2)}, u32[]{:S(2)}) collective-permute-start(f32[2,8,1536]{2,1,0:T(8,128)S(1)} %pad_maximum_fusion.3), channel_id=1, source_target_pairs={{0,2},{1,3},{2,0},{3,1},{4,6},{5,7},{6,4},{7,5},{8,10},{9,11},{10,... | collective-permute-start | bytes 294920 | tf_op jit(solution)/shard_map/ppermute | solution.py:353
  177.7 10.5 %collective-permute-start.29 = (f32[16,2,1536]{2,1,0:T(2,128)S(1)}, f32[16,2,1536]{2,1,0:T(2,128)S(1)}, u32[]{:S(2)}, u32[]{:S(2)}) collective-permute-start(f32[16,2,1536]{2,1,0:T(2,128)S(1)} %add.198), channel_id=1, source_target_pairs={{0,4},{1,5},{2,6},{3,7},{4,0},{5,1},{6,2},{7,3},{8,12},{9,13},{10,... | collective-permute-start | bytes 589832 | tf_op jit(solution)/shard_map/ppermute | solution.py:353
  178.8 10.5 %collective-permute-start.26 = (f32[4,8,1536]{2,1,0:T(8,128)S(1)}, f32[4,8,1536]{2,1,0:T(8,128)S(1)}, u32[]{:S(2)}, u32[]{:S(2)}) collective-permute-start(f32[4,8,1536]{2,1,0:T(8,128)S(1)} %pad_maximum_fusion.2), channel_id=1, source_target_pairs={{0,1},{1,0},{2,3},{3,2},{4,5},{5,4},{6,7},{7,6},{8,9},{9,8},{10,11... | collective-permute-start | bytes 589832 | tf_op jit(solution)/shard_map/ppermute | solution.py:353
  (9 other events, 266.5 us)
